TPU v7x, 256 devices: a whole 4x4x8 slice. The times are simulated.
256 devices in a mesh: energy: 64 (over x, y, z_lo, core), dom: 4 (over z_hi).
Axes of the slice: x: 4, y: 4, z: 8 (z_hi: 4, z_lo: 2; z = z_hi * 2 + z_lo), core: 2. Of those that a mesh axis runs over, the one named last changes fastest.
Arguments:
- pivots: float32 [64, 32, 320, 320], P('energy', 'dom'), may hold values from -0.0125 to 1.4125
- lower_spikes: float32 [64, 32, 320, 320], P('energy', 'dom'), may hold values from -0.0125 to 1.0025
- upper_spikes: float32 [64, 32, 320, 320], P('energy', 'dom'), may hold values from -0.0125 to 1.0025
- potential: float32 [32, 320, 320], P('dom', 'energy'), may hold values from -0.3125 to 0.3125
- grain_of_slice: int32 [32], P('dom'), may hold values from 0 to 31
- grain_shift: float32 [32], replicated, may hold values from 0.5 to 1.5
- probes: float32 [32, 320, 128], P('dom'), may hold values from -6 to 6
- weights: float32 [64], P('energy'), may hold values from 0.5 to 2
Outputs:
- response: float32 [32, 320], P('dom', 'energy')
All inputs are finite; a program needn't handle non-finite values.
Results may differ from a plain program's by a relative error of at most 0.00021.
Values sent between devices are 32-bit elements; how exact they have to be, the bound alone decides.
A program may use at most 128 MiB of HBM per device.

v0:
```python
import jax
import jax.numpy as jnp
from jax import lax
from jax.sharding import PartitionSpec as P

PROBES = 128


HIGHEST = lax.Precision.HIGHEST


def from_behind(x, axis, by):
    peers = lax.axis_size(axis)
    pairs = [(i, i + by) for i in range(peers) if 0 <= i + by < peers]
    return lax.ppermute(x, axis, pairs)


def sweep(blocks, given_rows, carried, backward):

    def sweep_advance(current, inputs_pair):
        matrix_block, given_value = inputs_pair
        current = given_value - jnp.dot(matrix_block, current, precision=HIGHEST)
        return (current, current)

    return lax.scan(sweep_advance, carried, (blocks, given_rows), reverse=backward)


def transfer(blocks, backward):
    orbitals = blocks.shape[1]

    def transfer_advance(current, matrix_block):
        return (-jnp.dot(matrix_block, current, precision=HIGHEST), None)

    result, _ = lax.scan(
        transfer_advance, jnp.eye(orbitals, dtype=jnp.float32), blocks, reverse=backward
    )
    return result


def boundary_value(matrix, offset, backward):
    zero_block = jnp.zeros(offset.shape, jnp.float32)
    inflow = zero_block
    direction = -1 if backward else 1
    for repeat in range(lax.axis_size("dom") - 1):
        outgoing = offset + jnp.dot(matrix, inflow, precision=HIGHEST)
        inflow = from_behind(outgoing, "dom", direction)
    return inflow


def solve(pivot_blocks, lower_blocks, upper_blocks, right_side, forward_map, backward_map):
    solved_pivot = jnp.einsum("sij,sjk->sik", pivot_blocks, right_side, precision=HIGHEST)
    zero_block = jnp.zeros(right_side.shape[1:], jnp.float32)
    last_local, _ = sweep(lower_blocks, solved_pivot, zero_block, False)
    inflow = boundary_value(forward_map, last_local, False)
    _, climbed = sweep(lower_blocks, solved_pivot, inflow, False)
    first_local, _ = sweep(upper_blocks, climbed, zero_block, True)
    outflow = boundary_value(backward_map, first_local, True)
    _, result = sweep(upper_blocks, climbed, outflow, True)
    return result


def per_device(
    pivots, lower_spikes, upper_spikes, potential, grain_of_slice, grain_shift, probes, weights
):
    pivot_blocks = pivots[0]
    lower_blocks = lower_spikes[0]
    upper_blocks = upper_spikes[0]
    grain_count = grain_shift.shape[0]
    grain_match = grain_of_slice[:, None] == jnp.arange(grain_count, dtype=jnp.int32)[None, :]
    grain_scale = jnp.sum(jnp.where(grain_match, grain_shift[None, :], 0.0), axis=1)
    gathered = lax.all_gather(potential, "energy", axis=1, tiled=True)
    perturb = gathered * grain_scale[:, None, None]
    forward_map = transfer(lower_blocks, False)
    backward_map = transfer(upper_blocks, True)
    first_solve = solve(pivot_blocks, lower_blocks, upper_blocks, probes, forward_map, backward_map)
    driven = jnp.einsum("sij,sjk->sik", perturb, first_solve, precision=HIGHEST)
    second_solve = solve(
        pivot_blocks, lower_blocks, upper_blocks, driven, forward_map, backward_map
    )
    energies = lax.axis_size("energy")
    charge_terms = weights[0] * jnp.sum(second_solve * probes, axis=2) / (PROBES * energies)
    return lax.psum_scatter(charge_terms, "energy", scatter_dimension=1, tiled=True)


def solution(mesh):
    placed = (
        P("energy", "dom", None, None),
        P("energy", "dom", None, None),
        P("energy", "dom", None, None),
        P("dom", "energy", None),
        P("dom"),
        P(),
        P("dom", None, None),
        P("energy"),
    )
    return jax.shard_map(
        per_device, mesh=mesh, in_specs=placed, out_specs=P("dom", "energy"), check_vma=False
    )
```

profile of v0, /device:TPU:1, one launch (start us, length us, event | category | flops | bytes accessed | tf_op | source)
XLA Modules:
  0.0 587.2 jit_solution(11058977467194568694)
XLA Ops:
  6.6 6.0 %fusion.48 = f32[8,320,128]{2,1,0:T(8,128)S(1)} fusion(f32[8,320,128]{2,1,0:T(8,128)} %param.34, f32[1,8,320,320]{3,2,1,0:T(8,128)} %param.28), kind=kOutput, calls=%fused_computation.62 | convolution fusion | flops 1258291200 | bytes 5898240 | tf_op jit(solution)/shard_map/sij,sjk->sik/dot_general | solution.py:51
  12.6 13.0 %while.138 = (s32[]{:T(128)}, f32[320,128]{1,0:T(8,128)S(1)}, f32[8,320,128]{2,1,0:T(8,128)S(1)}, f32[8,320,320]{2,1,0:T(8,128)}, s32[]{:T(128)}, /*index=5*/s32[]{:T(128)}) while((s32[]{:T(128)}, f32[320,128]{1,0:T(8,128)S(1)}, f32[8,320,128]{2,1,0:T(8,128)S(1)}, f32[8,320,320]{2,1,0:T(8,128)}, s32[]{:T(128)}, ...), condition=%wide.region_2.3_spmd.clone, body=%wide.region_1.2_spmd.clone.sunk | while | flops 157368320 | bytes 1311823 | solution.py:25
  26.7 17.4 %while.132 = (s32[]{:T(128)}, f32[320,320]{1,0:T(8,128)S(1)}, f32[8,320,320]{2,1,0:T(8,128)}, s32[]{:T(128)}) while((s32[]{:T(128)}, f32[320,320]{1,0:T(8,128)S(1)}, f32[8,320,320]{2,1,0:T(8,128)}, s32[]{:T(128)}) %tuple.278), condition=%wide.region_4.5_spmd, body=%wide.region_3.4_spmd.sunk | while | flops 393318400 | bytes 2130485 | solution.py:34
  26.8 2.1 convolution_negate_fusion.4
  28.9 2.1 convolution_negate_fusion.4
  31.1 2.1 convolution_negate_fusion.4
  33.3 2.1 convolution_negate_fusion.4
  35.5 2.1 convolution_negate_fusion.4
  37.7 2.1 convolution_negate_fusion.4
  39.8 2.1 convolution_negate_fusion.4
  42.0 2.1 convolution_negate_fusion.4
  44.7 5.7 collective-permute-start
  50.4 2.9 collective-permute-done
  53.9 9.6 %collective-permute-start.1 = (f32[320,128]{1,0:T(8,128)S(1)}, f32[320,128]{1,0:T(8,128)S(1)}, u32[]{:S(2)}, u32[]{:S(2)}) collective-permute-start(f32[320,128]{1,0:T(8,128)S(1)} %convolution_add_fusion.7), channel_id=1, source_target_pairs={{0,1},{1,2},{2,3},{4,5},{5,6},{6,7},{8,9},{9,10},{10,11},{12,13},{... | collective-permute-start | bytes 491528 | tf_op jit(solution)/shard_map/ppermute | solution.py:15
  63.5 2.2 collective-permute-done.1
  66.2 6.3 %collective-permute-start.2 = (f32[320,128]{1,0:T(8,128)S(1)}, f32[320,128]{1,0:T(8,128)S(1)}, u32[]{:S(2)}, u32[]{:S(2)}) collective-permute-start(f32[320,128]{1,0:T(8,128)S(1)} %convolution_add_fusion.6), channel_id=1, source_target_pairs={{0,1},{1,2},{2,3},{4,5},{5,6},{6,7},{8,9},{9,10},{10,11},{12,13},{... | collective-permute-start | bytes 491528 | tf_op jit(solution)/shard_map/ppermute | solution.py:15
  72.5 17.5 %while.134 = (s32[]{:T(128)}, f32[320,320]{1,0:T(8,128)S(1)}, f32[8,320,320]{2,1,0:T(8,128)}, s32[]{:T(128)}, s32[]{:T(128)}) while((s32[]{:T(128)}, f32[320,320]{1,0:T(8,128)S(1)}, f32[8,320,320]{2,1,0:T(8,128)}, s32[]{:T(128)}, s32[]{:T(128)}) %tuple.282), condition=%wide.region_10.11_spmd, body=%wide.region_9.10_spmd.sunk | while | flops 393318400 | bytes 2129997 | solution.py:34
  72.6 2.1 convolution_negate_fusion.5
  74.7 2.1 convolution_negate_fusion.5
  76.9 2.1 convolution_negate_fusion.5
  79.1 2.1 convolution_negate_fusion.5
  81.3 2.1 convolution_negate_fusion.5
  83.5 2.1 convolution_negate_fusion.5
  85.7 2.1 convolution_negate_fusion.5
  90.1 13.3 %while.133 = (s32[]{:T(128)}, f32[320,128]{1,0:T(8,128)S(1)}, f32[8,320,128]{2,1,0:T(8,128)S(1)}, f32[8,320,128]{2,1,0:T(8,128)}, f32[8,320,320]{2,1,0:T(8,128)}, /*index=5*/s32[]{:T(128)}) while((s32[]{:T(128)}, f32[320,128]{1,0:T(8,128)S(1)}, f32[8,320,128]{2,1,0:T(8,128)S(1)}, f32[8,320,128]{2,1,0:T(8,128)}, f32[8,320,320]{2,1,0:T(8,128)}, ...), condition=%wide.region_6.7_spmd, body=%wide.region_5.6_spmd.sunk | while | flops 157327360 | bytes 1475653 | solution.py:25
  103.4 13.0 %while.139 = (s32[]{:T(128)}, f32[320,128]{1,0:T(8,128)S(1)}, f32[8,320,128]{2,1,0:T(8,128)S(1)}, f32[8,320,320]{2,1,0:T(8,128)}, s32[]{:T(128)}, /*index=5*/s32[]{:T(128)}, s32[]{:T(128)}) while((s32[]{:T(128)}, f32[320,128]{1,0:T(8,128)S(1)}, f32[8,320,128]{2,1,0:T(8,128)S(1)}, f32[8,320,320]{2,1,0:T(8,128)}, s32[]{:T(128)}, ...), condition=%wide.region_8.9_spmd.clone, body=%wide.region_7.8_spmd.clone.sunk | while | flops 157368320 | bytes 1312354 | solution.py:25
  118.3 15.5 %collective-permute-done.3 = f32[320,128]{1,0:T(8,128)S(1)} collective-permute-done((f32[320,128]{1,0:T(8,128)S(1)}, f32[320,128]{1,0:T(8,128)S(1)}, u32[]{:S(2)}, u32[]{:S(2)}) %collective-permute-start.3) | collective-permute-done | bytes 163872 | tf_op jit(solution)/shard_map/ppermute | solution.py:15
  135.6 6.0 %collective-permute-done.4 = f32[320,128]{1,0:T(8,128)S(1)} collective-permute-done((f32[320,128]{1,0:T(8,128)S(1)}, f32[320,128]{1,0:T(8,128)S(1)}, u32[]{:S(2)}, u32[]{:S(2)}) %collective-permute-start.4) | collective-permute-done | bytes 163872 | tf_op jit(solution)/shard_map/ppermute | solution.py:15
  143.9 9.7 %collective-permute-done.5 = f32[320,128]{1,0:T(8,128)S(1)} collective-permute-done((f32[320,128]{1,0:T(8,128)S(1)}, f32[320,128]{1,0:T(8,128)S(1)}, u32[]{:S(2)}, u32[]{:S(2)}) %collective-permute-start.5) | collective-permute-done | bytes 163872 | tf_op jit(solution)/shard_map/ppermute | solution.py:15
  154.7 18.1 %while.135 = (s32[]{:T(128)}, f32[320,128]{1,0:T(8,128)S(1)}, f32[8,320,128]{2,1,0:T(8,128)}, f32[8,320,128]{2,1,0:T(8,128)S(1)}, f32[8,320,320]{2,1,0:T(8,128)}, /*index=5*/s32[]{:T(128)}, s32[]{:T(128)}) while((s32[]{:T(128)}, f32[320,128]{1,0:T(8,128)S(1)}, f32[8,320,128]{2,1,0:T(8,128)}, f32[8,320,128]{2,1,0:T(8,128)S(1)}, ...), condition=%wide.region_12.13_spmd, body=%wide.region_11.12_spmd.sunk | while | flops 157327360 | bytes 1475673 | solution.py:25
  154.8 2.3 bitcast_dynamic-update-slice_fusion.9
  157.0 2.2 bitcast_dynamic-update-slice_fusion.9
  159.3 2.2 bitcast_dynamic-update-slice_fusion.9
  161.5 2.2 bitcast_dynamic-update-slice_fusion.9
  163.8 2.2 bitcast_dynamic-update-slice_fusion.9
  166.1 2.2 bitcast_dynamic-update-slice_fusion.9
  168.3 2.2 bitcast_dynamic-update-slice_fusion.9
  170.6 2.2 bitcast_dynamic-update-slice_fusion.9
  172.8 2.8 all-gather.2.cloned.1.call-done
  175.6 2.4 broadcast_multiply_fusion
  178.1 4.2 fusion.50
  182.3 3.7 fusion.52
  186.0 13.0 %while.140 = (s32[]{:T(128)}, f32[320,128]{1,0:T(8,128)S(1)}, f32[8,320,128]{2,1,0:T(8,128)S(1)}, f32[8,320,320]{2,1,0:T(8,128)}, s32[]{:T(128)}, /*index=5*/s32[]{:T(128)}) while((s32[]{:T(128)}, f32[320,128]{1,0:T(8,128)S(1)}, f32[8,320,128]{2,1,0:T(8,128)S(1)}, f32[8,320,320]{2,1,0:T(8,128)}, s32[]{:T(128)}, ...), condition=%wide.region_14.15_spmd.clone, body=%wide.region_13.14_spmd.clone.sunk | while | flops 157368320 | bytes 1311823 | solution.py:25
  199.0 5.3 collective-permute-start.6
  204.4 3.3 collective-permute-done.6
  208.2 5.0 collective-permute-start.7
  213.3 2.2 collective-permute-done.7
  216.0 6.2 %collective-permute-start.8 = (f32[320,128]{1,0:T(8,128)S(1)}, f32[320,128]{1,0:T(8,128)S(1)}, u32[]{:S(2)}, u32[]{:S(2)}) collective-permute-start(f32[320,128]{1,0:T(8,128)S(1)} %convolution_add_fusion.2), channel_id=1, source_target_pairs={{0,1},{1,2},{2,3},{4,5},{5,6},{6,7},{8,9},{9,10},{10,11},{12,13},{... | collective-permute-start | bytes 491528 | tf_op jit(solution)/shard_map/ppermute | solution.py:15
  224.4 13.2 %while.136 = (s32[]{:T(128)}, f32[320,128]{1,0:T(8,128)S(1)}, f32[8,320,128]{2,1,0:T(8,128)S(1)}, f32[8,320,128]{2,1,0:T(8,128)}, f32[8,320,320]{2,1,0:T(8,128)}, /*index=5*/s32[]{:T(128)}) while((s32[]{:T(128)}, f32[320,128]{1,0:T(8,128)S(1)}, f32[8,320,128]{2,1,0:T(8,128)S(1)}, f32[8,320,128]{2,1,0:T(8,128)}, f32[8,320,320]{2,1,0:T(8,128)}, ...), condition=%wide.region_16.17_spmd, body=%wide.region_15.16_spmd.sunk | while | flops 157327360 | bytes 1475653 | solution.py:25
  237.6 13.0 %while.141 = (s32[]{:T(128)}, f32[320,128]{1,0:T(8,128)S(1)}, f32[8,320,128]{2,1,0:T(8,128)S(1)}, f32[8,320,320]{2,1,0:T(8,128)}, s32[]{:T(128)}, /*index=5*/s32[]{:T(128)}, s32[]{:T(128)}) while((s32[]{:T(128)}, f32[320,128]{1,0:T(8,128)S(1)}, f32[8,320,128]{2,1,0:T(8,128)S(1)}, f32[8,320,320]{2,1,0:T(8,128)}, s32[]{:T(128)}, ...), condition=%wide.region_18.19_spmd.clone, body=%wide.region_17.18_spmd.clone.sunk | while | flops 157368320 | bytes 1312354 | solution.py:25
  252.0 11.2 %collective-permute-done.9 = f32[320,128]{1,0:T(8,128)S(1)} collective-permute-done((f32[320,128]{1,0:T(8,128)S(1)}, f32[320,128]{1,0:T(8,128)S(1)}, u32[]{:S(2)}, u32[]{:S(2)}) %collective-permute-start.9) | collective-permute-done | bytes 163872 | tf_op jit(solution)/shard_map/ppermute | solution.py:15
  265.1 7.5 %collective-permute-done.10 = f32[320,128]{1,0:T(8,128)S(1)} collective-permute-done((f32[320,128]{1,0:T(8,128)S(1)}, f32[320,128]{1,0:T(8,128)S(1)}, u32[]{:S(2)}, u32[]{:S(2)}) %collective-permute-start.10) | collective-permute-done | bytes 163872 | tf_op jit(solution)/shard_map/ppermute | solution.py:15
  276.3 6.4 %collective-permute-done.11 = f32[320,128]{1,0:T(8,128)S(1)} collective-permute-done((f32[320,128]{1,0:T(8,128)S(1)}, f32[320,128]{1,0:T(8,128)S(1)}, u32[]{:S(2)}, u32[]{:S(2)}) %collective-permute-start.11) | collective-permute-done | bytes 163872 | tf_op jit(solution)/shard_map/ppermute | solution.py:15
  283.9 18.1 %while.137 = (s32[]{:T(128)}, f32[320,128]{1,0:T(8,128)S(1)}, f32[8,320,128]{2,1,0:T(8,128)}, f32[8,320,128]{2,1,0:T(8,128)S(1)}, f32[8,320,320]{2,1,0:T(8,128)}, /*index=5*/s32[]{:T(128)}, s32[]{:T(128)}) while((s32[]{:T(128)}, f32[320,128]{1,0:T(8,128)S(1)}, f32[8,320,128]{2,1,0:T(8,128)}, f32[8,320,128]{2,1,0:T(8,128)S(1)}, ...), condition=%wide.region_20.21_spmd, body=%wide.region_19.20_spmd.sunk | while | flops 157327360 | bytes 1475673 | solution.py:25
  283.9 2.2 bitcast_dynamic-update-slice_fusion.11
  286.1 2.2 bitcast_dynamic-update-slice_fusion.11
  288.4 2.2 bitcast_dynamic-update-slice_fusion.11
  290.7 2.2 bitcast_dynamic-update-slice_fusion.11
  292.9 2.3 bitcast_dynamic-update-slice_fusion.11
  295.2 2.2 bitcast_dynamic-update-slice_fusion.11
  297.5 2.2 bitcast_dynamic-update-slice_fusion.11
  299.7 2.2 bitcast_dynamic-update-slice_fusion.11
  302.0 2.2 multiply_reduce_fusion
  304.2 275.6 %all-reduce = f32[8,320]{1,0:T(8,128)S(1)} all-reduce(f32[8,320]{1,0:T(8,128)S(1)} %multiply_multiply_fusion), channel_id=2, replica_groups=mesh['energy'=64,'dom'=4] {'energy'}, use_global_device_ids=true, to_apply=%region_22.23.clone | all-reduce | flops 2560 | bytes 20480
  (179 shorter events, 100.6 us)
Async XLA Ops:
  6.5 169.1 %all-gather.2.cloned.1.call-start = ((), (), s32[]{:S(2)}) async-start(), calls=%async_computation | async-start | bytes 3993600 | tf_op jit(solution)/shard_map/all_gather | solution.py:71
  25.6 1.1 copy-start.1
  44.7 8.6 %collective-permute-start = (f32[320,128]{1,0:T(8,128)S(1)}, f32[320,128]{1,0:T(8,128)S(1)}, u32[]{:S(2)}, u32[]{:S(2)}) collective-permute-start(f32[320,128]{1,0:T(8,128)S(1)} %get-tuple-element.721), channel_id=1, source_target_pairs={{0,1},{1,2},{2,3},{4,5},{5,6},{6,7},{8,9},{9,10},{10,11},{12,13},{... | collective-permute-start | bytes 491528 | tf_op jit(solution)/shard_map/ppermute | solution.py:15
  53.9 11.8 %collective-permute-start.1 = (f32[320,128]{1,0:T(8,128)S(1)}, f32[320,128]{1,0:T(8,128)S(1)}, u32[]{:S(2)}, u32[]{:S(2)}) collective-permute-start(f32[320,128]{1,0:T(8,128)S(1)} %convolution_add_fusion.7), channel_id=1, source_target_pairs={{0,1},{1,2},{2,3},{4,5},{5,6},{6,7},{8,9},{9,10},{10,11},{12,13},{... | collective-permute-start | bytes 491528 | tf_op jit(solution)/shard_map/ppermute | solution.py:15
  66.2 23.8 %collective-permute-start.2 = (f32[320,128]{1,0:T(8,128)S(1)}, f32[320,128]{1,0:T(8,128)S(1)}, u32[]{:S(2)}, u32[]{:S(2)}) collective-permute-start(f32[320,128]{1,0:T(8,128)S(1)} %convolution_add_fusion.6), channel_id=1, source_target_pairs={{0,1},{1,2},{2,3},{4,5},{5,6},{6,7},{8,9},{9,10},{10,11},{12,13},{... | collective-permute-start | bytes 491528 | tf_op jit(solution)/shard_map/ppermute | solution.py:15
  116.4 27.3 %copy-start.4 = (f32[32]{0:T(128)S(1)}, f32[32]{0:T(128)}, u32[]{:S(2)}) copy-start(f32[32]{0:T(128)} %param.33) | copy-start | bytes 388
  116.4 27.3 %copy-start.5 = (s32[8]{0:T(128)S(1)}, s32[8]{0:T(128)}, u32[]{:S(2)}) copy-start(s32[8]{0:T(128)} %param.32) | copy-start | bytes 100
  117.0 16.8 %collective-permute-start.3 = (f32[320,128]{1,0:T(8,128)S(1)}, f32[320,128]{1,0:T(8,128)S(1)}, u32[]{:S(2)}, u32[]{:S(2)}) collective-permute-start(f32[320,128]{1,0:T(8,128)S(1)} %get-tuple-element.723), channel_id=1, source_target_pairs={{1,0},{2,1},{3,2},{5,4},{6,5},{7,6},{9,8},{10,9},{11,10},{13,12},{... | collective-permute-start | bytes 491528 | tf_op jit(solution)/shard_map/ppermute | solution.py:15
  134.3 7.3 %collective-permute-start.4 = (f32[320,128]{1,0:T(8,128)S(1)}, f32[320,128]{1,0:T(8,128)S(1)}, u32[]{:S(2)}, u32[]{:S(2)}) collective-permute-start(f32[320,128]{1,0:T(8,128)S(1)} %convolution_add_fusion.5), channel_id=1, source_target_pairs={{1,0},{2,1},{3,2},{5,4},{6,5},{7,6},{9,8},{10,9},{11,10},{13,12},{... | collective-permute-start | bytes 491528 | tf_op jit(solution)/shard_map/ppermute | solution.py:15
  142.2 11.4 %collective-permute-start.5 = (f32[320,128]{1,0:T(8,128)S(1)}, f32[320,128]{1,0:T(8,128)S(1)}, u32[]{:S(2)}, u32[]{:S(2)}) collective-permute-start(f32[320,128]{1,0:T(8,128)S(1)} %convolution_add_fusion.4), channel_id=1, source_target_pairs={{1,0},{2,1},{3,2},{5,4},{6,5},{7,6},{9,8},{10,9},{11,10},{13,12},{... | collective-permute-start | bytes 491528 | tf_op jit(solution)/shard_map/ppermute | solution.py:15
  172.8 5.2 copy-start.3
  178.1 4.2 copy-start
  199.0 23.3 %copy-start.2 = (f32[8,320,128]{2,1,0:T(8,128)}, f32[8,320,128]{2,1,0:T(8,128)S(1)}, u32[]{:S(2)}) copy-start(f32[8,320,128]{2,1,0:T(8,128)S(1)} %get-tuple-element.1198) | copy-start | bytes 3932164
  199.0 8.7 %collective-permute-start.6 = (f32[320,128]{1,0:T(8,128)S(1)}, f32[320,128]{1,0:T(8,128)S(1)}, u32[]{:S(2)}, u32[]{:S(2)}) collective-permute-start(f32[320,128]{1,0:T(8,128)S(1)} %add.139), channel_id=1, source_target_pairs={{0,1},{1,2},{2,3},{4,5},{5,6},{6,7},{8,9},{9,10},{10,11},{12,13},{... | collective-permute-start | bytes 491528 | tf_op jit(solution)/shard_map/ppermute | solution.py:15
  208.2 7.3 %collective-permute-start.7 = (f32[320,128]{1,0:T(8,128)S(1)}, f32[320,128]{1,0:T(8,128)S(1)}, u32[]{:S(2)}, u32[]{:S(2)}) collective-permute-start(f32[320,128]{1,0:T(8,128)S(1)} %convolution_add_fusion.3), channel_id=1, source_target_pairs={{0,1},{1,2},{2,3},{4,5},{5,6},{6,7},{8,9},{9,10},{10,11},{12,13},{... | collective-permute-start | bytes 491528 | tf_op jit(solution)/shard_map/ppermute | solution.py:15
  216.0 8.3 %collective-permute-start.8 = (f32[320,128]{1,0:T(8,128)S(1)}, f32[320,128]{1,0:T(8,128)S(1)}, u32[]{:S(2)}, u32[]{:S(2)}) collective-permute-start(f32[320,128]{1,0:T(8,128)S(1)} %convolution_add_fusion.2), channel_id=1, source_target_pairs={{0,1},{1,2},{2,3},{4,5},{5,6},{6,7},{8,9},{9,10},{10,11},{12,13},{... | collective-permute-start | bytes 491528 | tf_op jit(solution)/shard_map/ppermute | solution.py:15
  250.6 24.4 %copy-start.6 = (u32[256]{0:T(256)S(1)}, u32[256]{0:T(256)}, u32[]{:S(2)}) copy-start(u32[256]{0:T(256)} %constant.231) | copy-start | bytes 3076
  250.7 12.5 %collective-permute-start.9 = (f32[320,128]{1,0:T(8,128)S(1)}, f32[320,128]{1,0:T(8,128)S(1)}, u32[]{:S(2)}, u32[]{:S(2)}) collective-permute-start(f32[320,128]{1,0:T(8,128)S(1)} %add.142), channel_id=1, source_target_pairs={{1,0},{2,1},{3,2},{5,4},{6,5},{7,6},{9,8},{10,9},{11,10},{13,12},{... | collective-permute-start | bytes 491528 | tf_op jit(solution)/shard_map/ppermute | solution.py:15
  263.8 8.8 %collective-permute-start.10 = (f32[320,128]{1,0:T(8,128)S(1)}, f32[320,128]{1,0:T(8,128)S(1)}, u32[]{:S(2)}, u32[]{:S(2)}) collective-permute-start(f32[320,128]{1,0:T(8,128)S(1)} %convolution_add_fusion.1), channel_id=1, source_target_pairs={{1,0},{2,1},{3,2},{5,4},{6,5},{7,6},{9,8},{10,9},{11,10},{13,12},{... | collective-permute-start | bytes 491528 | tf_op jit(solution)/shard_map/ppermute | solution.py:15
  273.1 9.6 %collective-permute-start.11 = (f32[320,128]{1,0:T(8,128)S(1)}, f32[320,128]{1,0:T(8,128)S(1)}, u32[]{:S(2)}, u32[]{:S(2)}) collective-permute-start(f32[320,128]{1,0:T(8,128)S(1)} %convolution_add_fusion), channel_id=1, source_target_pairs={{1,0},{2,1},{3,2},{5,4},{6,5},{7,6},{9,8},{10,9},{11,10},{13,12},{... | collective-permute-start | bytes 491528 | tf_op jit(solution)/shard_map/ppermute | solution.py:15
Sparse Core Ops, SparseCore 0:
  63.6 112.0 all-gather.1
where the time goes:
time: 598 us; the launch traced here: 587 us
  blocking collectives  276 us (46%)
  matrix products  166 us (28%)
  waiting for transfers between devices  71.8 us (12%)
  starting transfers between devices  46.1 us (8%)
  between operations  15.1 us (3%)
  local copies, waits for them, and re-layouts  6.25 us (1%)
    unnamed x1, blocking collectives  276 us
    dot_general x64, matrix products, sweep_advance(): current = given_value - jnp.dot(matrix_block, current, precision=HIGHEST)  113 us
    ppermute x12, waiting for transfers between devices, from_behind(): return lax.ppermute(x, axis, pairs)  69 us
    ppermute x12, starting transfers between devices, from_behind(): return lax.ppermute(x, axis, pairs)  46.1 us
    dot_general x16, matrix products, transfer_advance(): return (-jnp.dot(matrix_block, current, precision=HIGHEST), None)  33.9 us
  transfers between devices with their start and end apart: 13, of which 12 were waited for; matrix products, arithmetic and copies ran while one was open for 11% of the time, Pallas kernels for 0%

commit v1 on v0

v1 whole, which is shorter than its diff:
```python
import functools

import jax
import jax.numpy as jnp
from jax import lax
from jax.experimental import pallas as pl
from jax.experimental.pallas import tpu as pltpu
from jax.sharding import PartitionSpec as P

MESH = pl.DeviceIdType.MESH
F32 = jnp.float32
BF16 = jnp.bfloat16
CHUNKS = 2


def split(x):
    high = x.astype(BF16)
    low = (x - high.astype(F32)).astype(BF16)
    return high, low


def dot(a, b):
    return jnp.dot(a, b, preferred_element_type=F32)


def product(a_high, a_low, x):
    high, low = split(x)
    n = x.shape[1]
    both = dot(a_high, jnp.concatenate([high, low], axis=1))
    return (both[:, :n] + both[:, n:]) + dot(a_low, high)


def kernel(
    grain_ref, shift_ref, weight_ref, potential_ref, pivots, lower, upper, probes,
    out_ref,
    raw, z_ref, mat_h, mat_l, phi, w_h, w_l, psi_h, psi_l, x_ref, c_ref, y_in, x_in,
    gathered, message, landing, charge, part_a, part_b,
    load_sem, z_sem, chain_send, chain_recv, gat_send, gat_recv, red_send, red_recv,
):
    slices, orbitals, columns = z_ref.shape
    energies = lax.axis_size("energy")
    e = lax.axis_index("energy")
    d = lax.axis_index("dom")
    core = lax.rem(e, 2)
    zl = lax.rem(e // 2, 2)
    y = lax.rem(e // 4, 4)
    x = e // 16

    def at(xx, yy, zz, cc):
        return (((xx * 4 + yy) * 2 + zz) * 2 + cc, d)

    def off(value, by, size):
        return lax.rem(value + by, size)

    group_a = [(i, j) for i in range(4) for j in range(2) if i or j]

    def peer_a(i, j):
        return at(off(x, i, 4), y, zl, off(core, j, 2))

    def peer_b(i, j):
        return at(x, off(y, i, 4), off(zl, j, 2), core)

    def load(source, which, s):
        return pltpu.make_async_copy(
            source.at[0, s], raw.at[which * slices + s], load_sem.at[which * slices + s]
        )

    z_copy = pltpu.make_async_copy(probes, z_ref, z_sem)
    load(pivots, 0, 0).start()
    load(lower, 1, 0).start()
    z_copy.start()
    for s in range(1, slices):
        load(pivots, 0, s).start()
        load(lower, 1, s).start()
    for s in reversed(range(slices)):
        load(upper, 2, s).start()

    barrier = pltpu.get_barrier_semaphore()
    for i, j in group_a:
        pl.semaphore_signal(barrier, inc=1, device_id=peer_a(i, j), device_id_type=MESH)
        pl.semaphore_signal(barrier, inc=1, device_id=peer_b(i, j), device_id_type=MESH)

    @pl.when(d > 0)
    def _():
        pl.semaphore_signal(barrier, inc=1, device_id=(e, d - 1), device_id_type=MESH)

    @pl.when(d < 3)
    def _():
        pl.semaphore_signal(barrier, inc=1, device_id=(e, d + 1), device_id_type=MESH)

    for s in range(slices):
        scale = shift_ref[grain_ref[s]]
        own = potential_ref[s] * scale
        for r in range(5):
            for t in range(3):
                piece = own[r : r + 1, 128 * t : min(128 * t + 128, orbitals)]
                gathered[t, x, y, zl, core, r * 8 + s : r * 8 + s + 1, 0 : piece.shape[1]] = piece

    @pl.when(jnp.logical_or(d == 0, d == 3))
    def _():
        pl.semaphore_wait(barrier, 2 * len(group_a) + 1)

    @pl.when(jnp.logical_and(d > 0, d < 3))
    def _():
        pl.semaphore_wait(barrier, 2 * len(group_a) + 2)

    def gather_copy(ref, slot, device):
        return pltpu.make_async_remote_copy(
            src_ref=ref, dst_ref=ref, send_sem=gat_send.at[slot], recv_sem=gat_recv.at[slot],
            device_id=device, device_id_type=MESH,
        )

    def stage_1():
        return [gather_copy(gathered.at[:, x, y, zl, core], 0, at(x, y, off(zl, 1, 2), core))]

    def along_x(ref, base):
        return [gather_copy(ref, base + k, at(off(x, k, 4), y, zl, core)) for k in (1, 2, 3)]

    def along_y(ref, base):
        return [gather_copy(ref, base + k, at(x, off(y, k, 4), zl, core)) for k in (1, 2, 3)]

    def stage_2(first):
        ref = gathered.at[:, x, y, :, core]
        return along_x(ref, 0) if first else along_y(ref, 0)

    def stage_3(first):
        if first:
            return along_y(gathered.at[:, :, y, :, core], 3)
        return along_x(gathered.at[:, x, :, :, core], 3)

    def stage_4():
        return [gather_copy(gathered.at[:, :, :, :, core], 7, at(x, y, zl, off(core, 1, 2)))]

    def on_core(action):
        @pl.when(core == 0)
        def _():
            action(True)

        @pl.when(core == 1)
        def _():
            action(False)

    def start_2(first):
        for copy in stage_2(first):
            copy.start()

    def start_3(first):
        for copy in stage_2(first):
            copy.wait_recv()
        for copy in stage_3(first):
            copy.start()

    def end_3(first):
        for copy in stage_3(first):
            copy.wait_recv()

    def end_sends(first):
        for copy in stage_2(first) + stage_3(first):
            copy.wait_send()

    stage_1()[0].start()

    half = columns // 2
    rows = orbitals // 2
    left = lax.broadcasted_iota(jnp.int32, (rows, columns), 1) < half

    def turn(v):
        return pltpu.roll(v, half, 1)

    def pack(v):
        return jnp.where(left, v[:rows], turn(v[rows:]))

    def unpack(m):
        return jnp.concatenate([m, turn(m)], axis=0)

    def join(v0, v1):
        wide = lax.broadcasted_iota(jnp.int32, (orbitals, columns), 1) < half
        return jnp.where(wide, v0, turn(v1))

    def chain_copy(step, c, device):
        slot = step * CHUNKS + c
        return pltpu.make_async_remote_copy(
            src_ref=message.at[slot], dst_ref=landing.at[slot],
            send_sem=chain_send.at[slot], recv_sem=chain_recv.at[slot],
            device_id=device, device_id_type=MESH,
        )

    def emit(step, c, value, device):
        message[step * CHUNKS + c] = pack(value)
        chain_copy(step, c, device).start()

    def emit_all(step, value, device):
        emit(step, 0, value, device)
        emit(step, 1, turn(value), device)

    def receive(step, c):
        chain_copy(step, c, (e, d)).wait_recv()
        return unpack(landing[step * CHUNKS + c])

    def relay(step, own, high, low, device, keep):
        v0 = receive(step, 0)
        emit(step, 0, own + product(high, low, v0), device)
        v1 = receive(step, 1)
        emit(step, 1, turn(own) + product(high, low, v1), device)
        keep[...] = join(v0, v1)

    def take(step, keep):
        v0 = receive(step, 0)
        keep[...] = join(v0, receive(step, 1))

    up = (e, d + 1)
    down = (e, d - 1)
    last = slices - 1

    def matrix(which, s):
        return mat_h[which * slices + s], mat_l[which * slices + s]

    def keep_split(which, s):
        high, low = split(raw[which * slices + s])
        mat_h[which * slices + s] = high
        mat_l[which * slices + s] = low

    z_copy.wait()
    load(pivots, 0, 0).wait()
    load(lower, 1, 0).wait()
    keep_split(0, 0)
    keep_split(1, 0)
    c_ref[0] = product(*matrix(0, 0), z_ref[0])

    def climb_first(s, _):
        load(pivots, 0, s).wait()
        load(lower, 1, s).wait()
        keep_split(0, s)
        keep_split(1, s)
        c = product(*matrix(0, s), z_ref[s])
        c_ref[s] = c - product(*matrix(1, s), c_ref[s - 1])
        return 0

    lax.fori_loop(1, slices, climb_first, 0)

    @pl.when(d == 0)
    def _():
        emit_all(0, c_ref[last], up)

    stage_1()[0].wait_recv()
    on_core(start_2)

    phi[0] = -raw[slices]

    def grow(s, _):
        phi[s] = -product(*matrix(1, s), phi[s - 1])
        return 0

    lax.fori_loop(1, slices, grow, 0)
    f_high, f_low = mat_h.at[3 * slices], mat_l.at[3 * slices]
    high, low = split(phi[last])
    f_high[...] = high
    f_low[...] = low
    on_core(start_3)

    def forward_relay(step):
        relay(step, c_ref[last], f_high[...], f_low[...], up, y_in)

    @pl.when(d == 1)
    def _():
        forward_relay(0)

    load(upper, 2, last).wait()
    keep_split(2, last)
    x_ref[last] = c_ref[last]
    w_h[last], w_l[last] = split(phi[last])
    psi = -raw[2 * slices + last]
    psi_h[last], psi_l[last] = split(psi)

    def product_of_pairs(a_high, a_low, high, low):
        n = high.shape[1]
        both = dot(a_high, jnp.concatenate([high, low], axis=1))
        return (both[:, :n] + both[:, n:]) + dot(a_low, high)

    def descend_first(k, _):
        s = last - k
        load(upper, 2, s).wait()
        keep_split(2, s)
        u = matrix(2, s)
        x_ref[s] = c_ref[s] - product(*u, x_ref[s + 1])
        w_h[s], w_l[s] = split(phi[s] - product_of_pairs(*u, w_h[s + 1], w_l[s + 1]))
        psi_h[s], psi_l[s] = split(-product_of_pairs(*u, psi_h[s + 1], psi_l[s + 1]))
        return 0

    lax.fori_loop(1, 4, descend_first, 0)

    @pl.when(d == 2)
    def _():
        forward_relay(0)

    lax.fori_loop(4, slices, descend_first, 0)

    def middle(step):
        @pl.when(d == 3)
        def _():
            take(step, y_in)

        @pl.when(d > 0)
        def _():
            x_ref[0] = x_ref[0] + product(w_h[0], w_l[0], y_in[...])

        @pl.when(d == 3)
        def _():
            emit_all(step + 1, x_ref[0], down)

        @pl.when(d > 0)
        def _():
            def spread(s, _):
                x_ref[s] = x_ref[s] + product(w_h[s], w_l[s], y_in[...])
                return 0

            lax.fori_loop(1, slices, spread, 0)

        @pl.when(jnp.logical_or(d == 1, d == 2))
        def _():
            relay(step + 1, x_ref[0], psi_h[0], psi_l[0], down, x_in)

        @pl.when(d == 0)
        def _():
            take(step + 1, x_in)

        @pl.when(d == 3)
        def _():
            x_in[...] = jnp.zeros_like(x_in)

    middle(0)
    on_core(end_3)
    stage_4()[0].start()
    stage_4()[0].wait_recv()

    flat = gathered.reshape(3 * energies * 40, 128)

    def drive(s, _):
        value = x_ref[s] + product(psi_h[s], psi_l[s], x_in[...])
        tiles = [flat[pl.ds(t * energies * 40 + s, orbitals, stride=8), :] for t in range(3)]
        tiles[2] = tiles[2][:, : orbitals - 256]
        block_high, block_low = split(jnp.concatenate(tiles, axis=1))
        driven = product(block_high, block_low, value)
        c_ref[s] = product(*matrix(0, s), driven)
        return 0

    lax.fori_loop(0, slices, drive, 0)

    def climb(s, _):
        c_ref[s] = c_ref[s] - product(*matrix(1, s), c_ref[s - 1])
        return 0

    lax.fori_loop(1, slices, climb, 0)

    @pl.when(d == 0)
    def _():
        emit_all(2, c_ref[last], up)

    @pl.when(jnp.logical_or(d == 1, d == 2))
    def _():
        forward_relay(2)

    x_ref[last] = c_ref[last]

    def descend(k, _):
        s = last - k
        x_ref[s] = c_ref[s] - product(*matrix(2, s), x_ref[s + 1])
        return 0

    lax.fori_loop(1, slices, descend, 0)
    middle(2)

    ones = jnp.ones((8, columns), BF16)
    factor = weight_ref[0] / (columns * energies)
    dims = (((1,), (1,)), ((), ()))

    def finish(s, _):
        value = x_ref[s] + product(psi_h[s], psi_l[s], x_in[...])
        high, low = split(value * z_ref[s])
        total = lax.dot_general(ones, high, dims, preferred_element_type=F32)
        total = total + lax.dot_general(ones, low, dims, preferred_element_type=F32)
        charge[pl.ds(s, 1), 0:orbitals] = total[0:1] * factor
        return 0

    charge[...] = jnp.zeros_like(charge)
    lax.fori_loop(0, slices, finish, 0)

    def exchange(source, parts, base, peer):
        copies = [
            pltpu.make_async_remote_copy(
                src_ref=source, dst_ref=parts.at[n], send_sem=red_send.at[base + n],
                recv_sem=red_recv.at[base + n], device_id=peer(i, j), device_id_type=MESH,
            )
            for n, (i, j) in enumerate(group_a)
        ]
        for copy in copies:
            copy.start()
        total = source[...]
        for n, copy in enumerate(copies):
            copy.wait_recv()
            total = total + parts[n]
        return total, copies

    total, sent_a = exchange(charge, part_a, 0, peer_a)
    part_b[7] = total
    total, sent_b = exchange(part_b.at[7], part_b, 7, peer_b)
    total = pltpu.roll(total, lax.rem(384 - 5 * e, 384), 1)
    out_ref[...] = total[:, :5]

    for copy in sent_a + sent_b + stage_1() + stage_4():
        copy.wait_send()
    on_core(end_sends)

    def chain_end(steps, device):
        for step in steps:
            for c in range(CHUNKS):
                chain_copy(step, c, device).wait_send()

    @pl.when(d < 3)
    def _():
        chain_end((0, 2), up)

    @pl.when(d > 0)
    def _():
        chain_end((1, 3), down)


def per_device(
    pivots, lower_spikes, upper_spikes, potential, grain_of_slice, grain_shift, probes, weights
):
    slices, orbitals, columns = probes.shape
    smem = pl.BlockSpec(memory_space=pltpu.SMEM)
    vmem = pl.BlockSpec(memory_space=pltpu.VMEM)
    hbm = pl.BlockSpec(memory_space=pl.ANY)
    dma = pltpu.SemaphoreType.DMA
    square = (slices, orbitals, orbitals)
    wide = (slices, orbitals, columns)
    return pl.pallas_call(
        kernel,
        out_shape=jax.ShapeDtypeStruct((slices, 5), F32),
        in_specs=[smem, smem, smem, vmem, hbm, hbm, hbm, hbm],
        out_specs=vmem,
        scratch_shapes=[
            pltpu.VMEM((3 * slices, orbitals, orbitals), F32),
            pltpu.VMEM(wide, F32),
            pltpu.VMEM((3 * slices + 1, orbitals, orbitals), BF16),
            pltpu.VMEM((3 * slices + 1, orbitals, orbitals), BF16),
            pltpu.VMEM(square, F32),
            pltpu.VMEM(square, BF16),
            pltpu.VMEM(square, BF16),
            pltpu.VMEM(square, BF16),
            pltpu.VMEM(square, BF16),
            pltpu.VMEM(wide, F32),
            pltpu.VMEM(wide, F32),
            pltpu.VMEM((orbitals, columns), F32),
            pltpu.VMEM((orbitals, columns), F32),
            pltpu.VMEM((3, 4, 4, 2, 2, 40, 128), F32),
            pltpu.VMEM((4 * CHUNKS, orbitals // CHUNKS, columns), F32),
            pltpu.VMEM((4 * CHUNKS, orbitals // CHUNKS, columns), F32),
            pltpu.VMEM((slices, 384), F32),
            pltpu.VMEM((7, slices, 384), F32),
            pltpu.VMEM((8, slices, 384), F32),
            dma((3 * slices,)),
            dma,
            dma((4 * CHUNKS,)),
            dma((4 * CHUNKS,)),
            dma((8,)),
            dma((8,)),
            dma((14,)),
            dma((14,)),
        ],
        compiler_params=pltpu.CompilerParams(
            collective_id=0, has_side_effects=True, vmem_limit_bytes=60 * 1024 * 1024
        ),
    )(grain_of_slice, grain_shift, weights, potential, pivots, lower_spikes, upper_spikes, probes)


def solution(mesh):
    placed = (
        P("energy", "dom", None, None),
        P("energy", "dom", None, None),
        P("energy", "dom", None, None),
        P("dom", "energy", None),
        P("dom"),
        P(),
        P("dom", None, None),
        P("energy"),
    )
    return jax.shard_map(
        per_device, mesh=mesh, in_specs=placed, out_specs=P("dom", "energy"), check_vma=False
    )
```

time: 598 us -> 123 us (0.21); the launches traced: 587 us -> 123 us
  blocking collectives: 276 us -> 0 us
  matrix products: 166 us -> 0 us
  Pallas kernels: 0 us -> 119 us
  waiting for transfers between devices: 71.8 us -> 0 us
  starting transfers between devices: 46.1 us -> 0 us
  between operations: 15.1 us -> 0.66 us
    unnamed x1 -> x0, blocking collectives: 276 us -> none
    dot_general x93 -> x0, matrix products: 166 us -> none  [the longest x64 113 us: sweep_advance(): current = given_value - jnp.dot(matrix_block, current, precision=HIGHEST)]
    pallas_call x0 -> x1, Pallas kernels: none -> 119 us  [per_device(): pl.pallas_call(kernel, out_shape=jax.ShapeDtypeStruct((slices, 5), F32),...]
    ppermute x12 -> x0, waiting for transfers between devices: 69 us -> none  [from_behind(): return lax.ppermute(x, axis, pairs)]
    ppermute x12 -> x0, starting transfers between devices: 46.1 us -> none  [from_behind(): return lax.ppermute(x, axis, pairs)]
  transfers between devices with their start and end apart: 13 -> 0, of which waited for: 12 -> 0; matrix products, arithmetic and copies ran while one was open for 11% -> 0% of each run, Pallas kernels for 0% -> 0%
where the time goes in v1:
time: 123 us
  Pallas kernels  119 us (97%)
  local copies, waits for them, and re-layouts  2.75 us (2%)
    pallas_call x1, Pallas kernels, per_device(): pl.pallas_call(kernel, out_shape=jax.ShapeDtypeStruct((slices, 5), F32),...  119 us
    unnamed x2, local copies, waits for them, and re-layouts  2.75 us

profile of v1, /device:TPU:1, one launch (start us, length us, event | category | flops | bytes accessed | tf_op | source)
XLA Modules:
  0.0 122.5 jit_solution(14186359867345710238)
XLA Ops:
  0.7 1.5 %copy.9.potential_ref = f32[8,5,320]{2,1,0:T(8,128)} copy(f32[8,5,320]{2,0,1:T(8,128)} %param.11) | data formatting | bytes 102400 | tf_op args[3]
  2.1 119.1 %shard_map.82 = f32[8,5]{1,0:T(8,128)} custom-call(s32[8]{0:T(128)} %grain_ref.1, f32[32]{0:T(128)} %shift_ref.1, f32[1]{0:T(128)S(6)} %copy.11.weight_ref, f32[8,5,320]{2,1,0:T(8,128)} %copy.9.potential_ref, f32[1,8,320,320]{3,2,1,0:T(8,128)} %pivots.1, f32[1,8,320,320]{3,2,1,0:T(8,128)} %lower.1, f32[1,8,320,320]{3,2,1,0:T(8,128)} %upper.1, ...), custom_call_target="tpu_custom_call" | custom-call | tf_op jit(solution)/shard_map/pallas_call | solution.py:438
  121.3 1.3 %copy.12 = f32[8,5]{1,0:T(8,128)} copy(f32[8,5]{1,0:T(8,128)} %shard_map.82) | data formatting | bytes 320

commit v2 on v1

--- a/solution.py
+++ b/solution.py
@@ -31,11 +31,12 @@
 
 
 def kernel(
-    grain_ref, shift_ref, weight_ref, potential_ref, pivots, lower, upper, probes,
+    grain_ref, shift_ref, weight_ref, potential, pivots, lower, upper, probes,
     out_ref,
+    potential_ref, reflect,
     raw, z_ref, mat_h, mat_l, phi, w_h, w_l, psi_h, psi_l, x_ref, c_ref, y_in, x_in,
     gathered, message, landing, charge, part_a, part_b,
-    load_sem, z_sem, chain_send, chain_recv, gat_send, gat_recv, red_send, red_recv,
+    load_sem, z_sem, chain_send, chain_recv, gat_send, gat_recv, red_send, red_recv, pot_sem, mat_send, mat_recv,
 ):
     slices, orbitals, columns = z_ref.shape
     energies = lax.axis_size("energy")
@@ -66,6 +67,8 @@
         )
 
     z_copy = pltpu.make_async_copy(probes, z_ref, z_sem)
+    pot_copy = pltpu.make_async_copy(potential, potential_ref, pot_sem)
+    pot_copy.start()
     load(pivots, 0, 0).start()
     load(lower, 1, 0).start()
     z_copy.start()
@@ -88,6 +91,7 @@
     def _():
         pl.semaphore_signal(barrier, inc=1, device_id=(e, d + 1), device_id_type=MESH)
 
+    pot_copy.wait()
     for s in range(slices):
         scale = shift_ref[grain_ref[s]]
         own = potential_ref[s] * scale
@@ -220,6 +224,27 @@
         mat_h[which * slices + s] = high
         mat_l[which * slices + s] = low
 
+    def loop(first, end, action, unroll=1):
+        lax.fori_loop(first, end, lambda s, carry: (action(s), carry)[1], 0, unroll=unroll)
+
+    def perturbation(s):
+        tiles = [flat[pl.ds(t * energies * 40 + s, orbitals, stride=8), :] for t in range(3)]
+        tiles[2] = tiles[2][:, : orbitals - 256]
+        return jnp.concatenate(tiles, axis=1)
+
+    flat = gathered.reshape(3 * energies * 40, 128)
+
+    def product_of_pairs(a_high, a_low, high, low):
+        n = high.shape[1]
+        both = dot(a_high, jnp.concatenate([high, low], axis=1))
+        return (both[:, :n] + both[:, n:]) + dot(a_low, high)
+
+    def is_dom(*which):
+        test = d == which[0]
+        for w in which[1:]:
+            test = jnp.logical_or(test, d == w)
+        return pl.when(test)
+
     z_copy.wait()
     load(pivots, 0, 0).wait()
     load(lower, 1, 0).wait()
@@ -227,163 +252,232 @@
     keep_split(1, 0)
     c_ref[0] = product(*matrix(0, 0), z_ref[0])
 
-    def climb_first(s, _):
+    def climb_first(s):
         load(pivots, 0, s).wait()
         load(lower, 1, s).wait()
         keep_split(0, s)
         keep_split(1, s)
         c = product(*matrix(0, s), z_ref[s])
         c_ref[s] = c - product(*matrix(1, s), c_ref[s - 1])
-        return 0
-
-    lax.fori_loop(1, slices, climb_first, 0)
-
-    @pl.when(d == 0)
-    def _():
-        emit_all(0, c_ref[last], up)
-
+
+    loop(1, 5, climb_first)
     stage_1()[0].wait_recv()
     on_core(start_2)
-
-    phi[0] = -raw[slices]
-
-    def grow(s, _):
+    loop(5, slices, climb_first)
+
+    f_high, f_low = mat_h.at[3 * slices], mat_l.at[3 * slices]
+
+    def grow(s):
         phi[s] = -product(*matrix(1, s), phi[s - 1])
-        return 0
-
-    lax.fori_loop(1, slices, grow, 0)
-    f_high, f_low = mat_h.at[3 * slices], mat_l.at[3 * slices]
-    high, low = split(phi[last])
-    f_high[...] = high
-    f_low[...] = low
-    on_core(start_3)
 
     def forward_relay(step):
         relay(step, c_ref[last], f_high[...], f_low[...], up, y_in)
 
-    @pl.when(d == 1)
-    def _():
-        forward_relay(0)
-
-    load(upper, 2, last).wait()
-    keep_split(2, last)
-    x_ref[last] = c_ref[last]
-    w_h[last], w_l[last] = split(phi[last])
-    psi = -raw[2 * slices + last]
-    psi_h[last], psi_l[last] = split(psi)
-
-    def product_of_pairs(a_high, a_low, high, low):
-        n = high.shape[1]
-        both = dot(a_high, jnp.concatenate([high, low], axis=1))
-        return (both[:, :n] + both[:, n:]) + dot(a_low, high)
-
-    def descend_first(k, _):
-        s = last - k
+    def descend_values(s):
+        x_ref[s] = c_ref[s] - product(*matrix(2, s), x_ref[s + 1])
+
+    def descend_w(s):
+        w_h[s], w_l[s] = split(phi[s] - product_of_pairs(*matrix(2, s), w_h[s + 1], w_l[s + 1]))
+
+    def descend_psi(s):
+        psi_h[s], psi_l[s] = split(-product_of_pairs(*matrix(2, s), psi_h[s + 1], psi_l[s + 1]))
+
+    def fetch_upper(s):
         load(upper, 2, s).wait()
         keep_split(2, s)
-        u = matrix(2, s)
-        x_ref[s] = c_ref[s] - product(*u, x_ref[s + 1])
-        w_h[s], w_l[s] = split(phi[s] - product_of_pairs(*u, w_h[s + 1], w_l[s + 1]))
-        psi_h[s], psi_l[s] = split(-product_of_pairs(*u, psi_h[s + 1], psi_l[s + 1]))
-        return 0
-
-    lax.fori_loop(1, 4, descend_first, 0)
-
-    @pl.when(d == 2)
+
+    def descend_first(with_w, with_psi):
+        def action(k):
+            s = last - k
+            fetch_upper(s)
+            descend_values(s)
+            if with_w:
+                descend_w(s)
+            if with_psi:
+                descend_psi(s)
+
+        return action
+
+    @is_dom(0)
+    def _():
+        emit_all(0, c_ref[last], up)
+
+    @is_dom(1, 2, 3)
+    def _():
+        phi[0] = -raw[slices]
+        loop(1, slices, grow)
+        w_h[last], w_l[last] = split(phi[last])
+        f_high[...] = w_h[last]
+        f_low[...] = w_l[last]
+
+    @is_dom(1)
     def _():
         forward_relay(0)
 
-    lax.fori_loop(4, slices, descend_first, 0)
-
-    def middle(step):
-        @pl.when(d == 3)
-        def _():
-            take(step, y_in)
-
-        @pl.when(d > 0)
-        def _():
-            x_ref[0] = x_ref[0] + product(w_h[0], w_l[0], y_in[...])
-
-        @pl.when(d == 3)
-        def _():
-            emit_all(step + 1, x_ref[0], down)
-
-        @pl.when(d > 0)
-        def _():
-            def spread(s, _):
-                x_ref[s] = x_ref[s] + product(w_h[s], w_l[s], y_in[...])
-                return 0
-
-            lax.fori_loop(1, slices, spread, 0)
-
-        @pl.when(jnp.logical_or(d == 1, d == 2))
-        def _():
-            relay(step + 1, x_ref[0], psi_h[0], psi_l[0], down, x_in)
-
-        @pl.when(d == 0)
-        def _():
-            take(step + 1, x_in)
-
-        @pl.when(d == 3)
-        def _():
-            x_in[...] = jnp.zeros_like(x_in)
-
-    middle(0)
-    on_core(end_3)
-    stage_4()[0].start()
-    stage_4()[0].wait_recv()
-
-    flat = gathered.reshape(3 * energies * 40, 128)
-
-    def drive(s, _):
+    on_core(start_3)
+    fetch_upper(last)
+    x_ref[last] = c_ref[last]
+    psi_h[last], psi_l[last] = split(-raw[2 * slices + last])
+
+    @is_dom(0)
+    def _():
+        loop(1, slices, descend_first(False, True))
+
+    @is_dom(1)
+    def _():
+        loop(1, slices, descend_first(True, True))
+
+    @is_dom(2)
+    def _():
+        loop(1, 4, descend_first(True, True))
+        forward_relay(0)
+        loop(4, slices, descend_first(True, True))
+
+    @is_dom(3)
+    def _():
+        loop(1, slices, descend_first(True, False))
+
+    def add_inflow(s):
+        x_ref[s] = x_ref[s] + product(w_h[s], w_l[s], y_in[...])
+
+    def end_gather():
+        on_core(end_3)
+        stage_4()[0].start()
+        stage_4()[0].wait_recv()
+
+    def reflect_copy(device):
+        return pltpu.make_async_remote_copy(
+            src_ref=phi.at[0], dst_ref=reflect, send_sem=mat_send, recv_sem=mat_recv,
+            device_id=device, device_id_type=MESH,
+        )
+
+    def backward_relay(step):
+        relay(step, x_ref[0], psi_h[0], psi_l[0], down, x_in)
+
+    @is_dom(3)
+    def _():
+        take(0, y_in)
+        add_inflow(0)
+        emit_all(1, x_ref[0], down)
+        phi[0] = w_h[0].astype(F32) + w_l[0].astype(F32)
+        reflect_copy(down).start()
+        loop(1, slices, add_inflow, 7)
+        x_in[...] = jnp.zeros_like(x_in)
+        end_gather()
+
+    @is_dom(2)
+    def _():
+        loop(0, slices, add_inflow, 4)
+        backward_relay(1)
+        end_gather()
+
+    @is_dom(1)
+    def _():
+        loop(0, slices, add_inflow, 4)
+        end_gather()
+        backward_relay(1)
+
+    @is_dom(0)
+    def _():
+        end_gather()
+        f_high[...] = jnp.zeros_like(f_high)
+        f_low[...] = jnp.zeros_like(f_low)
+        y_in[...] = jnp.zeros_like(y_in)
+
+        def fold(s):
+            joint = split(product_of_pairs(*matrix(0, s), *split(perturbation(s))))
+            given = product(*joint, x_ref[s])
+            reply = product_of_pairs(*joint, psi_h[s], psi_l[s])
+            y_in[...] = given - product(*matrix(1, s), y_in[...])
+            f_high[...], f_low[...] = split(
+                reply - product_of_pairs(*matrix(1, s), f_high[...], f_low[...])
+            )
+
+        loop(0, slices, fold)
+        v0 = receive(1, 0)
+        emit(2, 0, y_in[...] + product(f_high[...], f_low[...], v0), up)
+        v1 = receive(1, 1)
+        emit(2, 1, turn(y_in[...]) + product(f_high[...], f_low[...], v1), up)
+        x_in[...] = join(v0, v1)
+
+    def drive(s):
         value = x_ref[s] + product(psi_h[s], psi_l[s], x_in[...])
-        tiles = [flat[pl.ds(t * energies * 40 + s, orbitals, stride=8), :] for t in range(3)]
-        tiles[2] = tiles[2][:, : orbitals - 256]
-        block_high, block_low = split(jnp.concatenate(tiles, axis=1))
-        driven = product(block_high, block_low, value)
+        driven = product(*split(perturbation(s)), value)
         c_ref[s] = product(*matrix(0, s), driven)
-        return 0
-
-    lax.fori_loop(0, slices, drive, 0)
-
-    def climb(s, _):
+
+    def drive_last(s):
+        driven = product(*split(perturbation(s)), x_ref[s])
+        c_ref[s] = product(*matrix(0, s), driven)
+
+    @is_dom(0, 1, 2)
+    def _():
+        loop(0, slices, drive, 4)
+
+    @is_dom(3)
+    def _():
+        loop(0, slices, drive_last, 4)
+
+    def climb(s):
         c_ref[s] = c_ref[s] - product(*matrix(1, s), c_ref[s - 1])
-        return 0
-
-    lax.fori_loop(1, slices, climb, 0)
-
-    @pl.when(d == 0)
-    def _():
-        emit_all(2, c_ref[last], up)
-
-    @pl.when(jnp.logical_or(d == 1, d == 2))
+
+    loop(1, slices, climb)
+
+    @is_dom(1)
     def _():
         forward_relay(2)
 
     x_ref[last] = c_ref[last]
-
-    def descend(k, _):
-        s = last - k
-        x_ref[s] = c_ref[s] - product(*matrix(2, s), x_ref[s + 1])
-        return 0
-
-    lax.fori_loop(1, slices, descend, 0)
-    middle(2)
+    loop(1, slices, lambda k: descend_values(last - k))
+
+    @is_dom(3)
+    def _():
+        emit_all(3, x_ref[0], down)
+        take(2, y_in)
+        loop(0, slices, add_inflow, 4)
+
+    @is_dom(2)
+    def _():
+        reflect_copy((e, d)).wait_recv()
+        beyond = split(reflect[...])
+        answer = product(psi_h[0], psi_l[0], product_of_pairs(*beyond, f_high[...], f_low[...]))
+        answer = split(answer + (w_h[0].astype(F32) + w_l[0].astype(F32)))
+        take(3, x_in)
+        x_in[...] = x_in[...] + product(*beyond, c_ref[last])
+        own = x_ref[0] + product(psi_h[0], psi_l[0], x_in[...])
+        v0 = receive(2, 0)
+        emit(3, 0, own + product(*answer, v0), down)
+        v1 = receive(2, 1)
+        emit(3, 1, turn(own) + product(*answer, v1), down)
+        out0 = product(f_high[...], f_low[...], v0)
+        emit(2, 0, c_ref[last] + out0, up)
+        out1 = product(f_high[...], f_low[...], v1)
+        emit(2, 1, turn(c_ref[last]) + out1, up)
+        y_in[...] = join(v0, v1)
+        x_in[...] = x_in[...] + product(*beyond, join(out0, out1))
+        loop(0, slices, add_inflow, 4)
+
+    @is_dom(1)
+    def _():
+        loop(0, slices, add_inflow, 4)
+        backward_relay(3)
+
+    @is_dom(0)
+    def _():
+        take(3, x_in)
 
     ones = jnp.ones((8, columns), BF16)
     factor = weight_ref[0] / (columns * energies)
     dims = (((1,), (1,)), ((), ()))
 
-    def finish(s, _):
+    def finish(s):
         value = x_ref[s] + product(psi_h[s], psi_l[s], x_in[...])
         high, low = split(value * z_ref[s])
         total = lax.dot_general(ones, high, dims, preferred_element_type=F32)
         total = total + lax.dot_general(ones, low, dims, preferred_element_type=F32)
         charge[pl.ds(s, 1), 0:orbitals] = total[0:1] * factor
-        return 0
 
     charge[...] = jnp.zeros_like(charge)
-    lax.fori_loop(0, slices, finish, 0)
+    loop(0, slices, finish, 4)
 
     def exchange(source, parts, base, peer):
         copies = [
@@ -424,6 +518,10 @@
     def _():
         chain_end((1, 3), down)
 
+    @is_dom(3)
+    def _():
+        reflect_copy(down).wait_send()
+
 
 def per_device(
     pivots, lower_spikes, upper_spikes, potential, grain_of_slice, grain_shift, probes, weights
@@ -438,9 +536,11 @@
     return pl.pallas_call(
         kernel,
         out_shape=jax.ShapeDtypeStruct((slices, 5), F32),
-        in_specs=[smem, smem, smem, vmem, hbm, hbm, hbm, hbm],
+        in_specs=[smem, smem, smem, hbm, hbm, hbm, hbm, hbm],
         out_specs=vmem,
         scratch_shapes=[
+            pltpu.VMEM((slices, 5, orbitals), F32),
+            pltpu.VMEM((orbitals, orbitals), F32),
             pltpu.VMEM((3 * slices, orbitals, orbitals), F32),
             pltpu.VMEM(wide, F32),
             pltpu.VMEM((3 * slices + 1, orbitals, orbitals), BF16),
@@ -468,6 +568,9 @@
             dma((8,)),
             dma((14,)),
             dma((14,)),
+            dma,
+            dma,
+            dma,
         ],
         compiler_params=pltpu.CompilerParams(
             collective_id=0, has_side_effects=True, vmem_limit_bytes=60 * 1024 * 1024

time: 123 us -> 104 us (0.85)
  Pallas kernels: 119 us -> 101 us
    pallas_call x1, Pallas kernels: 119 us -> 101 us  [per_device(): pl.pallas_call(kernel, out_shape=jax.ShapeDtypeStruct((slices, 5), F32),...]
where the time goes in v2:
time: 104 us
  Pallas kernels  101 us (97%)
  local copies, waits for them, and re-layouts  2.75 us (3%)
    pallas_call x1, Pallas kernels, per_device(): pl.pallas_call(kernel, out_shape=jax.ShapeDtypeStruct((slices, 5), F32),...  101 us
    unnamed x2, local copies, waits for them, and re-layouts  2.75 us

profile of v2, /device:TPU:1, one launch (start us, length us, event | category | flops | bytes accessed | tf_op | source)
XLA Modules:
  0.0 104.3 jit_solution(16467089520484884353)
XLA Ops:
  0.7 1.5 %copy.9.potential = f32[8,5,320]{2,1,0:T(8,128)} copy(f32[8,5,320]{2,0,1:T(8,128)} %param.11) | data formatting | bytes 102400 | tf_op args[3]
  2.1 100.9 %shard_map.82 = f32[8,5]{1,0:T(8,128)} custom-call(s32[8]{0:T(128)} %grain_ref.1, f32[32]{0:T(128)} %shift_ref.1, f32[1]{0:T(128)S(6)} %copy.11.weight_ref, f32[8,5,320]{2,1,0:T(8,128)} %copy.9.potential, f32[1,8,320,320]{3,2,1,0:T(8,128)} %pivots.1, f32[1,8,320,320]{3,2,1,0:T(8,128)} %lower.1, f32[1,8,320,320]{3,2,1,0:T(8,128)} %upper.1, f32[8,320,128]{2,1,0:T(8,128)} %probes.1), custom_call_target="tpu_custom_call" | custom-call | tf_op jit(solution)/shard_map/pallas_call | solution.py:536
  103.0 1.3 %copy.12 = f32[8,5]{1,0:T(8,128)} copy(f32[8,5]{1,0:T(8,128)} %shard_map.82) | data formatting | bytes 320

commit v3 on v2

--- a/solution.py
+++ b/solution.py
@@ -33,7 +33,7 @@
 def kernel(
     grain_ref, shift_ref, weight_ref, potential, pivots, lower, upper, probes,
     out_ref,
-    potential_ref, reflect,
+    potential_ref, reflect_out, reflect,
     raw, z_ref, mat_h, mat_l, phi, w_h, w_l, psi_h, psi_l, x_ref, c_ref, y_in, x_in,
     gathered, message, landing, charge, part_a, part_b,
     load_sem, z_sem, chain_send, chain_recv, gat_send, gat_recv, red_send, red_recv, pot_sem, mat_send, mat_recv,
@@ -100,14 +100,6 @@
                 piece = own[r : r + 1, 128 * t : min(128 * t + 128, orbitals)]
                 gathered[t, x, y, zl, core, r * 8 + s : r * 8 + s + 1, 0 : piece.shape[1]] = piece
 
-    @pl.when(jnp.logical_or(d == 0, d == 3))
-    def _():
-        pl.semaphore_wait(barrier, 2 * len(group_a) + 1)
-
-    @pl.when(jnp.logical_and(d > 0, d < 3))
-    def _():
-        pl.semaphore_wait(barrier, 2 * len(group_a) + 2)
-
     def gather_copy(ref, slot, device):
         return pltpu.make_async_remote_copy(
             src_ref=ref, dst_ref=ref, send_sem=gat_send.at[slot], recv_sem=gat_recv.at[slot],
@@ -117,23 +109,29 @@
     def stage_1():
         return [gather_copy(gathered.at[:, x, y, zl, core], 0, at(x, y, off(zl, 1, 2), core))]
 
-    def along_x(ref, base):
-        return [gather_copy(ref, base + k, at(off(x, k, 4), y, zl, core)) for k in (1, 2, 3)]
-
-    def along_y(ref, base):
-        return [gather_copy(ref, base + k, at(x, off(y, k, 4), zl, core)) for k in (1, 2, 3)]
-
-    def stage_2(first):
-        ref = gathered.at[:, x, y, :, core]
-        return along_x(ref, 0) if first else along_y(ref, 0)
-
-    def stage_3(first):
+    def block(first, k):
         if first:
-            return along_y(gathered.at[:, :, y, :, core], 3)
-        return along_x(gathered.at[:, x, :, :, core], 3)
-
-    def stage_4():
-        return [gather_copy(gathered.at[:, :, :, :, core], 7, at(x, y, zl, off(core, 1, 2)))]
+            return gathered.at[:, off(x, 4 - k, 4), y, :, core]
+        return gathered.at[:, x, off(y, 4 - k, 4), :, core]
+
+    def line(first, k):
+        if first:
+            return gathered.at[:, :, off(y, 4 - k, 4), :, core]
+        return gathered.at[:, off(x, 4 - k, 4), :, :, core]
+
+    def ahead(along_x, k):
+        if along_x:
+            return at(off(x, k, 4), y, zl, core)
+        return at(x, off(y, k, 4), zl, core)
+
+    def stage_2(first, k):
+        return gather_copy(block(first, 0), k, ahead(first, k))
+
+    def stage_3(first, j, k):
+        return gather_copy(block(first, j), 4 * k + j, ahead(not first, k))
+
+    def stage_4(first, k):
+        return gather_copy(line(first, k), 16 + k, at(x, y, zl, off(core, 1, 2)))
 
     def on_core(action):
         @pl.when(core == 0)
@@ -144,25 +142,46 @@
         def _():
             action(False)
 
+    def forward_block(first, j):
+        for k in (1, 3, 2):
+            stage_3(first, j, k).start()
+
     def start_2(first):
-        for copy in stage_2(first):
-            copy.start()
+        for k in (1, 3, 2):
+            stage_2(first, k).start()
+        forward_block(first, 0)
 
     def start_3(first):
-        for copy in stage_2(first):
-            copy.wait_recv()
-        for copy in stage_3(first):
-            copy.start()
+        for j in (1, 3, 2):
+            stage_2(first, j).wait_recv()
+            forward_block(first, j)
+        stage_4(first, 0).start()
 
     def end_3(first):
-        for copy in stage_3(first):
-            copy.wait_recv()
+        for k in (1, 3, 2):
+            for j in range(4):
+                stage_3(first, j, k).wait_recv()
+            stage_4(first, k).start()
+        for k in range(4):
+            stage_4(first, k).wait_recv()
 
     def end_sends(first):
-        for copy in stage_2(first) + stage_3(first):
-            copy.wait_send()
-
-    stage_1()[0].start()
+        for k in (1, 2, 3):
+            stage_2(first, k).wait_send()
+            for j in range(4):
+                stage_3(first, j, k).wait_send()
+        for k in range(4):
+            stage_4(first, k).wait_send()
+
+    def gather_1():
+        stage_1()[0].wait_recv()
+        on_core(start_2)
+
+    def gather_2():
+        on_core(start_3)
+
+    def end_gather():
+        on_core(end_3)
 
     half = columns // 2
     rows = orbitals // 2
@@ -260,10 +279,17 @@
         c = product(*matrix(0, s), z_ref[s])
         c_ref[s] = c - product(*matrix(1, s), c_ref[s - 1])
 
-    loop(1, 5, climb_first)
-    stage_1()[0].wait_recv()
-    on_core(start_2)
-    loop(5, slices, climb_first)
+    loop(1, 4, climb_first)
+    @pl.when(jnp.logical_or(d == 0, d == 3))
+    def _():
+        pl.semaphore_wait(barrier, 2 * len(group_a) + 1)
+
+    @pl.when(jnp.logical_and(d > 0, d < 3))
+    def _():
+        pl.semaphore_wait(barrier, 2 * len(group_a) + 2)
+
+    stage_1()[0].start()
+    loop(4, slices, climb_first)
 
     f_high, f_low = mat_h.at[3 * slices], mat_l.at[3 * slices]
 
@@ -301,11 +327,14 @@
     @is_dom(0)
     def _():
         emit_all(0, c_ref[last], up)
+        gather_1()
 
     @is_dom(1, 2, 3)
     def _():
         phi[0] = -raw[slices]
-        loop(1, slices, grow)
+        loop(1, 4, grow)
+        gather_1()
+        loop(4, slices, grow)
         w_h[last], w_l[last] = split(phi[last])
         f_high[...] = w_h[last]
         f_low[...] = w_l[last]
@@ -314,40 +343,41 @@
     def _():
         forward_relay(0)
 
-    on_core(start_3)
     fetch_upper(last)
     x_ref[last] = c_ref[last]
     psi_h[last], psi_l[last] = split(-raw[2 * slices + last])
 
     @is_dom(0)
     def _():
-        loop(1, slices, descend_first(False, True))
+        loop(1, 5, descend_first(False, True))
+        gather_2()
+        loop(5, slices, descend_first(False, True))
 
     @is_dom(1)
     def _():
+        gather_2()
         loop(1, slices, descend_first(True, True))
 
     @is_dom(2)
     def _():
-        loop(1, 4, descend_first(True, True))
+        loop(1, 3, descend_first(True, True))
+        gather_2()
+        loop(3, 4, descend_first(True, True))
         forward_relay(0)
         loop(4, slices, descend_first(True, True))
 
     @is_dom(3)
     def _():
-        loop(1, slices, descend_first(True, False))
+        loop(1, 4, descend_first(True, False))
+        gather_2()
+        loop(4, slices, descend_first(True, False))
 
     def add_inflow(s):
         x_ref[s] = x_ref[s] + product(w_h[s], w_l[s], y_in[...])
 
-    def end_gather():
-        on_core(end_3)
-        stage_4()[0].start()
-        stage_4()[0].wait_recv()
-
     def reflect_copy(device):
         return pltpu.make_async_remote_copy(
-            src_ref=phi.at[0], dst_ref=reflect, send_sem=mat_send, recv_sem=mat_recv,
+            src_ref=reflect_out, dst_ref=reflect, send_sem=mat_send, recv_sem=mat_recv,
             device_id=device, device_id_type=MESH,
         )
 
@@ -356,12 +386,19 @@
 
     @is_dom(3)
     def _():
-        take(0, y_in)
-        add_inflow(0)
-        emit_all(1, x_ref[0], down)
-        phi[0] = w_h[0].astype(F32) + w_l[0].astype(F32)
+        w = w_h[0], w_l[0]
+        v0 = receive(0, 0)
+        emit(1, 0, x_ref[0] + product(*w, v0), down)
+        v1 = receive(0, 1)
+        emit(1, 1, turn(x_ref[0]) + product(*w, v1), down)
+        y_in[...] = join(v0, v1)
+        whole = w_h[0].astype(F32) + w_l[0].astype(F32)
+        reflect_out[:orbitals] = whole[:, :columns]
+        reflect_out[orbitals : 2 * orbitals] = whole[:, columns : 2 * columns]
+        rest = jnp.concatenate([whole[:, 2 * columns :], jnp.zeros((orbitals, half), F32)], axis=1)
+        reflect_out[2 * orbitals :] = pack(rest)
         reflect_copy(down).start()
-        loop(1, slices, add_inflow, 7)
+        loop(0, slices, add_inflow, 4)
         x_in[...] = jnp.zeros_like(x_in)
         end_gather()
 
@@ -374,8 +411,8 @@
     @is_dom(1)
     def _():
         loop(0, slices, add_inflow, 4)
+        backward_relay(1)
         end_gather()
-        backward_relay(1)
 
     @is_dom(0)
     def _():
@@ -393,7 +430,7 @@
                 reply - product_of_pairs(*matrix(1, s), f_high[...], f_low[...])
             )
 
-        loop(0, slices, fold)
+        loop(0, slices, fold, 2)
         v0 = receive(1, 0)
         emit(2, 0, y_in[...] + product(f_high[...], f_low[...], v0), up)
         v1 = receive(1, 1)
@@ -438,7 +475,9 @@
     @is_dom(2)
     def _():
         reflect_copy((e, d)).wait_recv()
-        beyond = split(reflect[...])
+        rest = unpack(reflect[2 * orbitals :])[:, :half]
+        whole = [reflect[:orbitals], reflect[orbitals : 2 * orbitals], rest]
+        beyond = split(jnp.concatenate(whole, axis=1))
         answer = product(psi_h[0], psi_l[0], product_of_pairs(*beyond, f_high[...], f_low[...]))
         answer = split(answer + (w_h[0].astype(F32) + w_l[0].astype(F32)))
         take(3, x_in)
@@ -501,7 +540,7 @@
     total = pltpu.roll(total, lax.rem(384 - 5 * e, 384), 1)
     out_ref[...] = total[:, :5]
 
-    for copy in sent_a + sent_b + stage_1() + stage_4():
+    for copy in sent_a + sent_b + stage_1():
         copy.wait_send()
     on_core(end_sends)
 
@@ -540,7 +579,8 @@
         out_specs=vmem,
         scratch_shapes=[
             pltpu.VMEM((slices, 5, orbitals), F32),
-            pltpu.VMEM((orbitals, orbitals), F32),
+            pltpu.VMEM((5 * orbitals // 2, columns), F32),
+            pltpu.VMEM((5 * orbitals // 2, columns), F32),
             pltpu.VMEM((3 * slices, orbitals, orbitals), F32),
             pltpu.VMEM(wide, F32),
             pltpu.VMEM((3 * slices + 1, orbitals, orbitals), BF16),
@@ -564,8 +604,8 @@
             dma,
             dma((4 * CHUNKS,)),
             dma((4 * CHUNKS,)),
-            dma((8,)),
-            dma((8,)),
+            dma((20,)),
+            dma((20,)),
             dma((14,)),
             dma((14,)),
             dma,

time: 104 us -> 99.2 us (0.954)
  Pallas kernels: 101 us -> 95.6 us
    pallas_call x1, Pallas kernels: 101 us -> 95.6 us  [per_device(): pl.pallas_call(kernel, out_shape=jax.ShapeDtypeStruct((slices, 5), F32),...]
where the time goes in v3:
time: 99.2 us; the launch traced here: 99 us
  Pallas kernels  95.6 us (96%)
  local copies, waits for them, and re-layouts  2.75 us (3%)
    pallas_call x1, Pallas kernels, per_device(): pl.pallas_call(kernel, out_shape=jax.ShapeDtypeStruct((slices, 5), F32),...  95.6 us
    unnamed x2, local copies, waits for them, and re-layouts  2.75 us

profile of v3, /device:TPU:1, one launch (start us, length us, event | category | flops | bytes accessed | tf_op | source)
XLA Modules:
  0.0 99.0 jit_solution(11763675399141586751)
XLA Ops:
  0.7 1.5 %copy.9.potential = f32[8,5,320]{2,1,0:T(8,128)} copy(f32[8,5,320]{2,0,1:T(8,128)} %param.11) | data formatting | bytes 102400 | tf_op args[3]
  2.1 95.6 %shard_map.82 = f32[8,5]{1,0:T(8,128)} custom-call(s32[8]{0:T(128)} %grain_ref.1, f32[32]{0:T(128)} %shift_ref.1, f32[1]{0:T(128)S(6)} %copy.11.weight_ref, f32[8,5,320]{2,1,0:T(8,128)} %copy.9.potential, f32[1,8,320,320]{3,2,1,0:T(8,128)} %pivots.1, f32[1,8,320,320]{3,2,1,0:T(8,128)} %lower.1, f32[1,8,320,320]{3,2,1,0:T(8,128)} %upper.1, f32[8,320,128]{2,1,0:T(8,128)} %probes.1), custom_call_target="tpu_custom_call" | custom-call | tf_op jit(solution)/shard_map/pallas_call | solution.py:575
  97.7 1.3 %copy.12 = f32[8,5]{1,0:T(8,128)} copy(f32[8,5]{1,0:T(8,128)} %shard_map.82) | data formatting | bytes 320

commit v4 on v3

--- a/solution.py
+++ b/solution.py
@@ -392,14 +392,14 @@
         v1 = receive(0, 1)
         emit(1, 1, turn(x_ref[0]) + product(*w, v1), down)
         y_in[...] = join(v0, v1)
+        loop(0, slices, add_inflow, 4)
+        x_in[...] = jnp.zeros_like(x_in)
         whole = w_h[0].astype(F32) + w_l[0].astype(F32)
         reflect_out[:orbitals] = whole[:, :columns]
         reflect_out[orbitals : 2 * orbitals] = whole[:, columns : 2 * columns]
         rest = jnp.concatenate([whole[:, 2 * columns :], jnp.zeros((orbitals, half), F32)], axis=1)
         reflect_out[2 * orbitals :] = pack(rest)
         reflect_copy(down).start()
-        loop(0, slices, add_inflow, 4)
-        x_in[...] = jnp.zeros_like(x_in)
         end_gather()
 
     @is_dom(2)

time: 99.2 us -> 99.3 us (level)
  no operation moved by 1% of the time
where the time goes in v4:
time: 99.3 us; the launch traced here: 99.2 us
  Pallas kernels  95.8 us (96%)
  local copies, waits for them, and re-layouts  2.75 us (3%)
    pallas_call x1, Pallas kernels, per_device(): pl.pallas_call(kernel, out_shape=jax.ShapeDtypeStruct((slices, 5), F32),...  95.8 us
    unnamed x2, local copies, waits for them, and re-layouts  2.75 us

profile of v4, /device:TPU:1, one launch (start us, length us, event | category | flops | bytes accessed | tf_op | source)
XLA Modules:
  0.0 99.2 jit_solution(10956632773290803066)
XLA Ops:
  0.7 1.5 %copy.9.potential = f32[8,5,320]{2,1,0:T(8,128)} copy(f32[8,5,320]{2,0,1:T(8,128)} %param.11) | data formatting | bytes 102400 | tf_op args[3]
  2.1 95.8 %shard_map.82 = f32[8,5]{1,0:T(8,128)} custom-call(s32[8]{0:T(128)} %grain_ref.1, f32[32]{0:T(128)} %shift_ref.1, f32[1]{0:T(128)S(6)} %copy.11.weight_ref, f32[8,5,320]{2,1,0:T(8,128)} %copy.9.potential, f32[1,8,320,320]{3,2,1,0:T(8,128)} %pivots.1, f32[1,8,320,320]{3,2,1,0:T(8,128)} %lower.1, f32[1,8,320,320]{3,2,1,0:T(8,128)} %upper.1, f32[8,320,128]{2,1,0:T(8,128)} %probes.1), custom_call_target="tpu_custom_call" | custom-call | tf_op jit(solution)/shard_map/pallas_call | solution.py:575
  97.9 1.3 %copy.12 = f32[8,5]{1,0:T(8,128)} copy(f32[8,5]{1,0:T(8,128)} %shard_map.82) | data formatting | bytes 320
